TPU v7x, 32 devices: a whole 2x2x4 slice. The times are simulated.
32 devices in a mesh: dp: 8 (over y, x, core), narrow: 4 (over z).
Axes of the slice: x: 2, y: 2, z: 4, core: 2. Of those that a mesh axis runs over, the one named last changes fastest.
Arguments:
- tokens: bfloat16 [4, 8, 512, 768], P('narrow', 'dp'), may hold values from -6 to 6
- cotangent: bfloat16 [4, 8, 512, 768], P('narrow', 'dp'), may hold values from -6 to 6
- resets: int32 [4, 8], P(None, 'dp'), may hold values 0 or 1
- truncation: int32 [4], replicated, may hold values from 1 to 8
- memory_state: float32 [4, 768, 2304], P(None, None, 'narrow'), may hold values from -192 to 192
- normalizer: float32 [4, 2304], P(None, 'narrow'), may hold values from 0.5 to 2
- query_weight: bfloat16 [768, 384], P(('dp', 'narrow')), may hold values from -0.21875 to 0.21875
- key_weight: bfloat16 [768, 384], P(('dp', 'narrow')), may hold values from -0.21875 to 0.21875
- value_weight: bfloat16 [768, 768], P(('dp', 'narrow')), may hold values from -1.75 to 1.75
- gate_weight: bfloat16 [768], P(('dp', 'narrow')), may hold values from -0.21875 to 0.21875
- first_gain: bfloat16 [768], P(('dp', 'narrow')), may hold values from 0.5 to 1.5
- mixing_weight: bfloat16 [768, 2304], P(('dp', 'narrow')), may hold values from -0.21875 to 0.21875
- output_weight: bfloat16 [768, 768], P(('dp', 'narrow')), may hold values from -0.875 to 0.875
- second_gain: bfloat16 [768], P(('dp', 'narrow')), may hold values from 0.5 to 1.5
- expand_weight: bfloat16 [768, 3072], P(('dp', 'narrow')), may hold values from -0.21875 to 0.21875
- reduce_weight: bfloat16 [3072, 768], P(('dp', 'narrow')), may hold values from -0.109375 to 0.109375
Outputs:
- block_out: bfloat16 [4, 8, 512, 768], P('narrow', 'dp')
- token_grad: float32 [4, 8, 512, 768], P('narrow', 'dp')
- query_grad: float32 [768, 384], P(('dp', 'narrow'))
- key_grad: float32 [768, 384], P(('dp', 'narrow'))
- value_grad: float32 [768, 768], P(('dp', 'narrow'))
- gate_grad: float32 [768], P(('dp', 'narrow'))
- first_grad: float32 [768], P(('dp', 'narrow'))
- mixing_grad: float32 [768, 2304], P(('dp', 'narrow'))
- output_grad: float32 [768, 768], P(('dp', 'narrow'))
- second_grad: float32 [768], P(('dp', 'narrow'))
- expand_grad: float32 [768, 3072], P(('dp', 'narrow'))
- reduce_grad: float32 [3072, 768], P(('dp', 'narrow'))
Inputs may be any that keep to these rules, and one draw needn't show every extreme that they name: `resets`: 1 marks a segment that begins a new document: its memory read ignores everything written before it. Gradients reach the memory writes of the last truncation[s] segments of stream s only.
All inputs are finite; a program needn't handle non-finite values. No bound on the sum of `resets` on one device may be relied on, other than what follows from the above.
Results may differ from a plain program's by a relative error of at most 0.02.
Values may be sent and summed in bfloat16 or wider, within the bound.
A program may use at most 512 MiB of HBM per device.

v0:
```python
import jax
import jax.numpy as jnp
from jax import lax
from jax.sharding import PartitionSpec as P

HEADS = 12
HD = 64
MEM = 16


exact_mode = lax.Precision.HIGHEST
ln_eps = 1e-05
masked_score = -1e30
bf_type = jnp.bfloat16
float_kind = jnp.float32


def carried_in(value, axis, join, neutral):
    place = lax.axis_index(axis)
    gathered = jax.tree.map(
        lambda a, kind: lax.all_gather(a.astype(kind), axis),
        value,
        (jnp.bfloat16, jnp.bfloat16, jnp.bfloat16),
    )
    state = jax.tree.map(lambda a, e: jnp.zeros_like(a) + jnp.asarray(e, a.dtype), value, neutral)

    def carried_one(turn, state):
        return join(
            state,
            jax.tree.map(
                lambda a, own: lax.dynamic_index_in_dim(a, turn, 0, False).astype(own.dtype),
                gathered,
                value,
            ),
        )

    return lax.fori_loop(0, place, carried_one, state)


def entering(value, axis, join, neutral):
    count = lax.axis_size(axis)
    place = lax.axis_index(axis)
    ahead = count - 1 - place
    gathered = jax.tree.map(
        lambda a, kind: lax.all_gather(a.astype(kind), axis),
        value,
        jax.tree.map(lambda a: jnp.bfloat16 if a.dtype == jnp.float32 else a.dtype, value),
    )
    state = jax.tree.map(lambda a, e: jnp.zeros_like(a) + jnp.asarray(e, a.dtype), value, neutral)

    def entering_one(turn, state):
        source = count - 1 - turn
        return join(
            state,
            jax.tree.map(
                lambda a, own: lax.dynamic_index_in_dim(a, source, 0, False).astype(own.dtype),
                gathered,
                value,
            ),
        )

    return lax.fori_loop(0, ahead, entering_one, state)


def matmul(left, right):
    return jnp.dot(left, right, preferred_element_type=float_kind)


def rounded(values):
    return lax.optimization_barrier(values.astype(bf_type)).astype(float_kind)


def halves_of(inputs):
    return jnp.concatenate([jax.nn.relu(inputs), jax.nn.relu(-inputs)], axis=-1)


def column_features(inputs, first_idx, second_idx):
    halves = halves_of(inputs)
    return jnp.take(halves, first_idx, axis=-1) * jnp.take(halves, second_idx, axis=-1)


def own_columns(key_width, col_count):
    first_col = lax.axis_index("narrow") * col_count
    columns = first_col + jnp.arange(col_count, dtype=jnp.int32)
    within = columns % (2 * key_width)
    block_num = columns // (2 * key_width)
    partner = (within - block_num - 1) % (2 * key_width)
    return (within, partner)


def norm_forward(inputs, gain):
    center = inputs - jnp.mean(inputs, axis=-1, keepdims=True)
    inv_std = lax.rsqrt(jnp.mean(center * center, axis=-1, keepdims=True) + ln_eps)
    unit = center * inv_std
    return (unit * gain, unit, inv_std)


def norm_backward(grad_out, unit, inv_std, gain):
    grad_unit = grad_out * gain
    grad_gain = jnp.sum(grad_out * unit, axis=0)
    grad_in = inv_std * (
        grad_unit
        - jnp.mean(grad_unit, axis=-1, keepdims=True)
        - unit * jnp.mean(grad_unit * unit, axis=-1, keepdims=True)
    )
    return (grad_in, grad_gain)


def chain(earlier, later):
    keep_early, memory_early, normal_early = earlier
    keep_late, memory_late, normalizer_final = later
    return (
        keep_early * keep_late,
        memory_early * keep_late[:, None, None] + memory_late,
        normal_early * keep_late[:, None] + normalizer_final,
    )


def block_scores(query_blk, key_seg, row_start):
    raw = jnp.einsum(
        "qhd,khd->hqk", query_blk, key_seg, preferred_element_type=float_kind
    ) * query_blk.shape[-1] ** (-0.5)
    rows_pos = row_start + jnp.arange(query_blk.shape[0])
    cols_pos = jnp.arange(key_seg.shape[0])
    return jnp.where((cols_pos[None, :] <= rows_pos[:, None])[None], raw, masked_score)


def body(
    tokens,
    cotangent,
    resets,
    truncation,
    memory_state,
    normalizer,
    query_weight,
    key_weight,
    value_weight,
    gate_weight,
    first_gain,
    mixing_weight,
    output_weight,
    second_gain,
    expand_weight,
    reduce_weight,
):
    query_w, key_w, value_w, gate_w, gain_one, mixing_w, output_w, gain_two, expand_w, reduce_w = (
        lax.all_gather(query_weight, ("dp", "narrow"), axis=0, tiled=True),
        lax.all_gather(key_weight, ("dp", "narrow"), axis=0, tiled=True),
        lax.all_gather(value_weight, ("dp", "narrow"), axis=0, tiled=True),
        lax.all_gather(gate_weight, ("dp", "narrow"), axis=0, tiled=True),
        lax.all_gather(first_gain, ("dp", "narrow"), axis=0, tiled=True),
        lax.all_gather(mixing_weight, ("dp", "narrow"), axis=0, tiled=True),
        lax.all_gather(output_weight, ("dp", "narrow"), axis=0, tiled=True),
        lax.all_gather(second_gain, ("dp", "narrow"), axis=0, tiled=True),
        lax.all_gather(expand_weight, ("dp", "narrow"), axis=0, tiled=True),
        lax.all_gather(reduce_weight, ("dp", "narrow"), axis=0, tiled=True),
    )
    seg_count = tokens.shape[0]
    seg_len = tokens.shape[2]
    width = tokens.shape[3]
    row_count = seg_count * seg_len
    key_width = query_w.shape[1]
    stream_count = memory_state.shape[0]
    col_count = memory_state.shape[2]
    gain_one_f = gain_one.astype(float_kind)
    gain_two_f = gain_two.astype(float_kind)
    tok_rows = tokens.reshape(row_count, width)
    memory_rows = tokens[:, 0, seg_len - MEM :, :].reshape(seg_count * MEM, width)
    mem_query = matmul(tok_rows, query_w).astype(bf_type)
    write_keys = matmul(memory_rows, key_w).astype(bf_type)
    write_vals = matmul(memory_rows, value_w).astype(bf_type)
    gate_prob = jax.nn.sigmoid(matmul(memory_rows, gate_w))
    gate_low = gate_prob.astype(bf_type)
    first_idx, second_idx = own_columns(key_width, col_count)
    keep_flag = 1.0 - resets[:, 0].astype(float_kind)
    all_query, all_keys, all_vals, all_gates = (
        lax.all_gather(mem_query, "narrow", axis=0, tiled=True),
        lax.all_gather(write_keys, "narrow", axis=0, tiled=True),
        lax.all_gather(write_vals, "narrow", axis=0, tiled=True),
        lax.all_gather(gate_low, "narrow", axis=0, tiled=True),
    )
    key_feat = rounded(column_features(all_keys.astype(float_kind), first_idx, second_idx)).reshape(
        stream_count, MEM, col_count
    )
    gates_f = all_gates.astype(float_kind).reshape(stream_count, MEM, 1)
    vals_f = all_vals.astype(float_kind).reshape(stream_count, MEM, width)
    scaled_vals = vals_f * gates_f
    delta = jnp.einsum("smd,smc->sdc", scaled_vals, key_feat, precision=exact_mode)
    delta_norm = jnp.sum(key_feat, axis=1)
    identity = (jnp.ones_like(keep_flag), jnp.zeros_like(delta), jnp.zeros_like(delta_norm))
    prod_keep, acc_memory, acc_normal = carried_in(
        (keep_flag, delta, delta_norm), "dp", chain, identity
    )
    memory_now = keep_flag[:, None, None] * (prod_keep[:, None, None] * memory_state + acc_memory)
    normal_now = keep_flag[:, None] * (prod_keep[:, None] * normalizer + acc_normal)
    query_features = (
        column_features(all_query.astype(float_kind), first_idx, second_idx)
        .astype(bf_type)
        .reshape(stream_count, seg_len, col_count)
    )
    memory_reduced_precision = memory_now.astype(bf_type)
    part_num = jnp.einsum(
        "nuz,nwz->nuw", query_features, memory_reduced_precision, preferred_element_type=float_kind
    ).reshape(stream_count * seg_len, width)
    part_den = jnp.einsum(
        "slc,sc->sl", query_features.astype(float_kind), normal_now, precision=exact_mode
    ).reshape(stream_count * seg_len)
    numerator, den_sum = (
        lax.psum_scatter(
            part_num.astype(jnp.bfloat16), "narrow", scatter_dimension=0, tiled=True
        ).astype(jnp.float32),
        lax.psum_scatter(
            part_den.astype(jnp.bfloat16), "narrow", scatter_dimension=0, tiled=True
        ).astype(jnp.float32),
    )
    den_total = 1.0 + den_sum
    first_res = tok_rows.astype(float_kind) + numerator / den_total[:, None]
    normed_one, unit_one, inv_one = norm_forward(first_res, gain_one_f)
    normed_one_low = normed_one.astype(bf_type)
    mixed = matmul(normed_one_low, mixing_w)
    queries = mixed[:, :width].astype(bf_type).reshape(seg_count, seg_len, HEADS, HD)
    key_heads = mixed[:, width : 2 * width].astype(bf_type).reshape(seg_count, seg_len, HEADS, HD)
    head_values = mixed[:, 2 * width :].astype(bf_type).reshape(seg_count, seg_len, HEADS, HD)
    block_rows = min(seg_len, 512)
    block_count = seg_len // block_rows

    def attend(flat_idx):
        seg_idx = flat_idx // block_count
        row_start = flat_idx % block_count * block_rows
        query_seg = lax.dynamic_index_in_dim(queries, seg_idx, 0, keepdims=False)
        key_seg = lax.dynamic_index_in_dim(key_heads, seg_idx, 0, keepdims=False)
        value_seg = lax.dynamic_index_in_dim(head_values, seg_idx, 0, keepdims=False)
        scores = block_scores(query_seg, key_seg, row_start)
        top_score = jnp.max(scores, axis=-1, keepdims=True)
        raw_weights = jnp.exp(scores - top_score)
        exp_total = jnp.sum(raw_weights, axis=-1, keepdims=True)
        log_total = top_score[..., 0] + jnp.log(exp_total[..., 0])
        probs = (raw_weights / exp_total).astype(bf_type)
        attended_blk = jnp.einsum(
            "hqk,khd->qhd", probs, value_seg, preferred_element_type=float_kind
        ).astype(bf_type)
        return (attended_blk, log_total)

    attended, log_totals = lax.map(attend, jnp.arange(seg_count * block_count, dtype=jnp.int32))
    attended_rows = attended.reshape(row_count, width)
    log_totals = log_totals.reshape(seg_count, block_count, HEADS, block_rows)
    branch = matmul(attended_rows, output_w)
    second_res = first_res + branch
    normed_two, unit_two, inv_two = norm_forward(second_res, gain_two_f)
    normed_two_low = normed_two.astype(bf_type)
    expanded = matmul(normed_two_low, expand_w)
    activated_low = jax.nn.gelu(expanded, approximate=True).astype(bf_type)
    reduced = matmul(activated_low, reduce_w)
    block_out = (second_res + reduced).astype(bf_type).reshape(seg_count, 1, seg_len, width)
    grad_block = cotangent.reshape(row_count, width)
    grad_reduce = matmul(activated_low.T, grad_block)
    grad_act = matmul(grad_block, reduce_w.T)
    unused, gelu_pull = jax.vjp(lambda inputs: jax.nn.gelu(inputs, approximate=True), expanded)
    grad_expanded = gelu_pull(grad_act)[0].astype(bf_type)
    grad_expand = matmul(normed_two_low.T, grad_expanded)
    grad_normed_two = matmul(grad_expanded, expand_w.T)
    grad_in_two, grad_gain_two = norm_backward(grad_normed_two, unit_two, inv_two, gain_two_f)
    grad_second = grad_block.astype(float_kind) + grad_in_two
    grad_branch = grad_second.astype(bf_type)
    grad_output = matmul(attended_rows.T, grad_branch)
    grad_att = (
        matmul(grad_branch, output_w.T).astype(bf_type).reshape(seg_count, seg_len, HEADS, HD)
    )

    def attend_back(items):
        query_seg, key_seg, value_seg, grad_seg, log_seg = items
        score_scale = query_seg.shape[-1] ** (-0.5)
        scores = block_scores(query_seg, key_seg, 0)
        probs = jnp.exp(scores - log_seg[0][:, :, None])
        grad_value = jnp.einsum(
            "hqk,qhd->khd", probs.astype(bf_type), grad_seg, preferred_element_type=float_kind
        )
        grad_probs = jnp.einsum(
            "qhd,khd->hqk", grad_seg, value_seg, preferred_element_type=float_kind
        )
        grad_scores = (
            probs * (grad_probs - jnp.sum(probs * grad_probs, axis=-1, keepdims=True))
        ).astype(bf_type)
        query_parts = [
            (
                jnp.einsum("hqk,khd->qhd", grad_scores, key_seg, preferred_element_type=float_kind)
                * score_scale
            ).astype(bf_type)
        ]
        grad_key = (
            jnp.einsum("hqk,qhd->khd", grad_scores, query_seg, preferred_element_type=float_kind)
            * score_scale
        )
        return (
            jnp.concatenate(query_parts, axis=0),
            grad_key.astype(bf_type),
            grad_value.astype(bf_type),
        )

    grad_queries, grad_keys, grad_values = lax.map(
        attend_back, (queries, key_heads, head_values, grad_att, log_totals)
    )
    grad_mixed = jnp.concatenate(
        [
            grad_queries.reshape(row_count, width),
            grad_keys.reshape(row_count, width),
            grad_values.reshape(row_count, width),
        ],
        axis=1,
    )
    grad_mixing = matmul(normed_one_low.T, grad_mixed)
    grad_normed_one = matmul(grad_mixed, mixing_w.T)
    grad_in_one, grad_gain_one = norm_backward(grad_normed_one, unit_one, inv_one, gain_one_f)
    grad_first = grad_second + grad_in_one
    grad_num = (grad_first / den_total[:, None]).astype(bf_type)
    grad_den = (-jnp.sum(grad_first * numerator, axis=-1) / (den_total * den_total)).astype(bf_type)
    all_gnum, all_gden = (
        lax.all_gather(grad_num, "narrow", axis=0, tiled=True),
        lax.all_gather(grad_den, "narrow", axis=0, tiled=True),
    )
    gate_numerator_segment = all_gnum.reshape(stream_count, seg_len, width)
    gden_seg = all_gden.astype(float_kind).reshape(stream_count, seg_len)
    grad_feat = (
        jnp.einsum(
            "ait,ato->aio",
            gate_numerator_segment,
            memory_reduced_precision,
            preferred_element_type=float_kind,
        )
        + gden_seg[:, :, None] * normal_now[:, None, :]
    )
    memory_gradient = jnp.einsum(
        "nkj,nkg->njg", gate_numerator_segment, query_features, preferred_element_type=float_kind
    )
    grad_normal = jnp.einsum(
        "sl,slc->sc", gden_seg, query_features.astype(float_kind), precision=exact_mode
    )
    unused, feat_pull = jax.vjp(
        lambda inputs: column_features(inputs, first_idx, second_idx), all_query.astype(float_kind)
    )
    query_part = feat_pull(grad_feat.reshape(stream_count * seg_len, col_count))[0]
    backward_entries = (
        keep_flag,
        keep_flag[:, None, None] * memory_gradient,
        keep_flag[:, None] * grad_normal,
    )
    unused_keep, grad_delta, grad_delta_norm = entering(backward_entries, "dp", chain, identity)
    live = (lax.axis_index("dp") >= lax.axis_size("dp") - truncation).astype(float_kind)
    grad_delta = grad_delta * live[:, None, None]
    grad_delta_norm = grad_delta_norm * live[:, None]
    grad_scaled = jnp.einsum("sdc,smc->smd", grad_delta, key_feat, precision=exact_mode)
    vals_part = (grad_scaled * gates_f).reshape(stream_count * MEM, width)
    gates_part = jnp.sum(grad_scaled * vals_f, axis=-1).reshape(stream_count * MEM)
    grad_kfeat = (
        jnp.einsum("smd,sdc->smc", scaled_vals, grad_delta, precision=exact_mode)
        + grad_delta_norm[:, None, :]
    )
    unused, key_pull = jax.vjp(
        lambda inputs: column_features(inputs, first_idx, second_idx), all_keys.astype(float_kind)
    )
    keys_part = key_pull(grad_kfeat.reshape(stream_count * MEM, col_count))[0]
    grad_mq, grad_wk, grad_wv, grad_gate = (
        lax.psum_scatter(
            query_part.astype(jnp.bfloat16), "narrow", scatter_dimension=0, tiled=True
        ).astype(jnp.float32),
        lax.psum_scatter(
            keys_part.astype(jnp.bfloat16), "narrow", scatter_dimension=0, tiled=True
        ).astype(jnp.float32),
        lax.psum_scatter(
            vals_part.astype(jnp.bfloat16), "narrow", scatter_dimension=0, tiled=True
        ).astype(jnp.float32),
        lax.psum_scatter(
            gates_part.astype(jnp.bfloat16), "narrow", scatter_dimension=0, tiled=True
        ).astype(jnp.float32),
    )
    grad_mq_low = grad_mq.astype(bf_type)
    grad_wk_low = grad_wk.astype(bf_type)
    grad_wv_low = grad_wv.astype(bf_type)
    grad_logit = grad_gate.astype(bf_type).astype(float_kind) * gate_prob * (1.0 - gate_prob)
    token_rows = grad_first + matmul(grad_mq_low, query_w.T)
    memory_extra = (
        matmul(grad_wk_low, key_w.T)
        + matmul(grad_wv_low, value_w.T)
        + grad_logit[:, None] * gate_w.astype(float_kind)[None, :]
    )
    token_seg = token_rows.reshape(seg_count, seg_len, width)
    token_seg = token_seg.at[:, seg_len - MEM :, :].add(memory_extra.reshape(seg_count, MEM, width))
    token_grad = token_seg.reshape(seg_count, 1, seg_len, width)
    grad_query = matmul(tok_rows.T, grad_mq_low)
    grad_key = matmul(memory_rows.T, grad_wk_low)
    grad_value = matmul(memory_rows.T, grad_wv_low)
    grad_gate_w = jnp.dot(memory_rows.astype(float_kind).T, grad_logit, precision=exact_mode)
    summed = (
        lax.psum_scatter(grad_query, ("dp", "narrow"), scatter_dimension=0, tiled=True),
        lax.psum_scatter(grad_key, ("dp", "narrow"), scatter_dimension=0, tiled=True),
        lax.psum_scatter(grad_value, ("dp", "narrow"), scatter_dimension=0, tiled=True),
        lax.psum_scatter(grad_gate_w, ("dp", "narrow"), scatter_dimension=0, tiled=True),
        lax.psum_scatter(grad_gain_one, ("dp", "narrow"), scatter_dimension=0, tiled=True),
        lax.psum_scatter(grad_mixing, ("dp", "narrow"), scatter_dimension=0, tiled=True),
        lax.psum_scatter(grad_output, ("dp", "narrow"), scatter_dimension=0, tiled=True),
        lax.psum_scatter(grad_gain_two, ("dp", "narrow"), scatter_dimension=0, tiled=True),
        lax.psum_scatter(grad_expand, ("dp", "narrow"), scatter_dimension=0, tiled=True),
        lax.psum_scatter(grad_reduce, ("dp", "narrow"), scatter_dimension=0, tiled=True),
    )
    return (
        block_out,
        token_grad,
        summed[0],
        summed[1],
        summed[2],
        summed[3],
        summed[4],
        summed[5],
        summed[6],
        summed[7],
        summed[8],
        summed[9],
    )


def solution(mesh):
    placed = (
        P("narrow", "dp", None, None),
        P("narrow", "dp", None, None),
        P(None, "dp"),
        P(),
        P(None, None, "narrow"),
        P(None, "narrow"),
        P(("dp", "narrow"), None),
        P(("dp", "narrow"), None),
        P(("dp", "narrow"), None),
        P(("dp", "narrow")),
        P(("dp", "narrow")),
        P(("dp", "narrow"), None),
        P(("dp", "narrow"), None),
        P(("dp", "narrow")),
        P(("dp", "narrow"), None),
        P(("dp", "narrow"), None),
    )
    return jax.shard_map(
        body,
        mesh=mesh,
        in_specs=placed,
        out_specs=(
            P("narrow", "dp", None, None),
            P("narrow", "dp", None, None),
            P(("dp", "narrow"), None),
            P(("dp", "narrow"), None),
            P(("dp", "narrow"), None),
            P(("dp", "narrow")),
            P(("dp", "narrow")),
            P(("dp", "narrow"), None),
            P(("dp", "narrow"), None),
            P(("dp", "narrow")),
            P(("dp", "narrow"), None),
            P(("dp", "narrow"), None),
        ),
        check_vma=False,
    )
```

profile of v0, /device:TPU:0, one launch (start us, length us, event | category | flops | bytes accessed | tf_op | source)
XLA Modules:
  0.0 2127.4 jit_solution(13134898499000641577)
XLA Ops:
  8.0 75.2 %all_gather.76 = bf16[768,384]{1,0:T(8,128)(2,1)S(1)} all-gather(bf16[24,384]{1,0:T(8,128)(2,1)} %param.36), channel_id=1, replica_groups=mesh['dp'=8,'narrow'=4] {'dp','narrow'}, dimensions={0}, use_global_device_ids=true | all-gather | bytes 608256 | tf_op jit(solution)/shard_map/all_gather | solution.py:147
  86.6 73.1 %all_gather.83 = bf16[768,384]{1,0:T(8,128)(2,1)S(1)} all-gather(bf16[24,384]{1,0:T(8,128)(2,1)} %param.37), channel_id=1, replica_groups=mesh['dp'=8,'narrow'=4] {'dp','narrow'}, dimensions={0}, use_global_device_ids=true | all-gather | bytes 608256 | tf_op jit(solution)/shard_map/all_gather | solution.py:148
  160.6 13.1 all_gather.84
  179.0 37.7 %all-reduce.14 = (bf16[768]{0:T(1024)(128)(2,1)S(1)}, bf16[768]{0:T(1024)(128)(2,1)}, bf16[768]{0:T(1024)(128)(2,1)}) all-reduce(bf16[768]{0:T(1024)(128)(2,1)S(1)} %dynamic-update-slice.5, bf16[768]{0:T(1024)(128)(2,1)S(1)} %dynamic-update-slice.7, ...), channel_id=1, replica_groups=mesh['dp'=8,'narrow'=4] {'dp','narrow'}, use_global_device_ids=true, to_apply=%add.1 | all-reduce | flops 2304 | bytes 9216
  219.6 10.5 all-reduce.2
  231.7 13.3 all_gather.80
  252.1 11.9 all-reduce
  264.8 11.7 all-gather.5
  288.0 9.5 gather_fusion.1
  297.4 9.5 gather_fusion
  306.9 8.5 fusion.25
  315.4 72.1 %all-gather.32.cloned.1.call-done = bf16[32,768,576]{1,2,0:T(8,128)(2,1)} async-done(((bf16[4,768,576]{1,2,0:T(8,128)(2,1)}), bf16[32,768,576]{1,2,0:T(8,128)(2,1)}) %all-gather.32.cloned.1.call-update) | async-done | bytes 28311568 | tf_op jit(solution)/shard_map/all_gather | solution.py:21
  391.2 8.8 copy.140
  417.1 11.7 all-reduce.5
  428.9 156.3 %reduce-scatter.14.cloned.1.call-done = bf16[512,768]{1,0:T(8,128)(2,1)} async-done(((bf16[2048,768]{1,0:T(8,128)(2,1)}), bf16[512,768]{1,0:T(8,128)(2,1)}) %reduce-scatter.14.cloned.1.call-update) | async-done | bytes 786448 | tf_op jit(solution)/shard_map/reduce_scatter | solution.py:209
  588.5 59.5 %all-gather.22.cloned.1.call-done = bf16[768,2304]{1,0:T(8,128)(2,1)} async-done(((bf16[24,2304]{1,0:T(8,128)(2,1)}), bf16[768,2304]{1,0:T(8,128)(2,1)}) %all-gather.22.cloned.1.call-update) | async-done | bytes 3538960 | tf_op jit(solution)/shard_map/all_gather | solution.py:152
  665.7 37.8 %all-gather.24.cloned.1.call-done = bf16[768,768]{1,0:T(8,128)(2,1)} async-done(((bf16[24,768]{1,0:T(8,128)(2,1)}), bf16[768,768]{1,0:T(8,128)(2,1)}) %all-gather.24.cloned.1.call-update) | async-done | bytes 1179664 | tf_op jit(solution)/shard_map/all_gather | solution.py:153
  706.3 62.5 %all-gather.26.cloned.1.call-done = bf16[768,3072]{1,0:T(8,128)(2,1)} async-done(((bf16[24,3072]{1,0:T(8,128)(2,1)}), bf16[768,3072]{1,0:T(8,128)(2,1)}) %all-gather.26.cloned.1.call-update) | async-done | bytes 4718608 | tf_op jit(solution)/shard_map/all_gather | solution.py:155
  775.8 57.7 %all-gather.28.cloned.1.call-done = bf16[3072,768]{1,0:T(8,128)(2,1)} async-done(((bf16[96,768]{1,0:T(8,128)(2,1)}), bf16[3072,768]{1,0:T(8,128)(2,1)}) %all-gather.28.cloned.1.call-update) | async-done | bytes 4718608 | tf_op jit(solution)/shard_map/all_gather | solution.py:156
  833.6 8.7 fusion.16
  855.8 9.6 multiply_reduce_fusion
  884.9 12.8 all-gather.6
  897.7 47.2 %all-gather.30.cloned.1.call-done = bf16[2048,768]{1,0:T(8,128)(2,1)} async-done(((bf16[512,768]{1,0:T(8,128)(2,1)}), bf16[2048,768]{1,0:T(8,128)(2,1)}) %all-gather.30.cloned.1.call-update) | async-done | bytes 3145744 | tf_op jit(solution)/shard_map/all_gather | solution.py:318
  952.6 20.4 scatter_custom_fusion
  979.5 20.2 scatter_custom_fusion.1
  1022.0 10.1 all-gather.7
  1032.1 16.1 reduce-scatter.16.cloned.1.call-done
  1050.7 136.8 %all-gather.34.cloned.1.call-done = bf16[32,768,576]{1,2,0:T(8,128)(2,1)} async-done(((bf16[4,768,576]{1,2,0:T(8,128)(2,1)}), bf16[32,768,576]{1,2,0:T(8,128)(2,1)}) %all-gather.34.cloned.1.call-update) | async-done | bytes 28311568 | tf_op jit(solution)/shard_map/all_gather | solution.py:45
  1191.1 111.1 %while.9 = (s32[]{:T(128)}, f32[4,768,576]{2,1,0:T(8,128)}, f32[4,576]{1,0:T(4,128)S(1)}, s32[]{:T(128)}, bf16[8,4]{1,0:T(8,128)(2,1)}, /*index=5*/bf16[8,4,768,...) while((s32[]{:T(128)}, f32[4,768,576]{2,1,0:T(8,128)}, ...), condition=%wide.region_21.26_spmd, body=%wide.region_20.25_spmd.sunk | while | flops 5315338 | bytes 31873768 | solution.py:62
  1197.9 8.3 convert_add_fusion.11
  1213.8 8.3 convert_add_fusion.11
  1229.6 8.3 convert_add_fusion.11
  1245.5 8.3 convert_add_fusion.11
  1261.4 8.3 convert_add_fusion.11
  1277.3 8.3 convert_add_fusion.11
  1293.1 8.3 convert_add_fusion.11
  1325.9 7.9 fusion.94
  1333.9 10.3 reduce-scatter.18.cloned.1.call-done
  1366.7 9.6 fusion.76
  1383.1 9.1 fusion.62
  1394.0 8.8 all-reduce.6
  1403.1 40.4 %all-reduce.12 = (f32[768]{0:T(1024)S(1)}, f32[768]{0:T(1024)S(1)}, f32[768]{0:T(1024)S(1)}) all-reduce(f32[768]{0:T(1024)S(1)} %convolution_reduce_fusion, f32[768]{0:T(1024)S(1)} %copy-done.80, f32[768]{0:T(1024)S(1)} %copy-done.79), channel_id=16, replica_groups=mesh['dp'=8,'narrow'=4] {'dp','narrow'}, use_global_device_ids=true, to_apply=%region_31.36.clone | all-reduce | flops 2304 | bytes 18432
  1447.9 56.4 %all-reduce.17.cloned.1.call-done = (f32[768,384]{0,1:T(8,128)}, f32[768,384]{0,1:T(8,128)}) async-done(((f32[768,384]{0,1:T(8,128)}, f32[768,384]{0,1:T(8,128)}), (f32[768,384]{0,1:T(8,128)}, f32[768,384]{0,1:T(8,128)})) %all-reduce.17.cloned.1.call-update) | async-done | bytes 2359312
  1508.0 100.6 %reduce-scatter.24.cloned.1.call-done = f32[24,768]{1,0:T(8,128)} async-done(((f32[768,768]{1,0:T(8,128)}), f32[24,768]{1,0:T(8,128)}) %reduce-scatter.24.cloned.1.call-update) | async-done | bytes 73744 | tf_op jit(solution)/shard_map/reduce_scatter | solution.py:400
  1608.6 124.8 %reduce-scatter.22.cloned.1.call-done = f32[24,2304]{1,0:T(8,128)} async-done(((f32[768,2304]{1,0:T(8,128)}), f32[24,2304]{1,0:T(8,128)}) %reduce-scatter.22.cloned.1.call-update) | async-done | bytes 221200 | tf_op jit(solution)/shard_map/reduce_scatter | solution.py:399
  1733.4 141.3 %reduce-scatter.26.cloned.1.call-done = f32[24,3072]{1,0:T(8,128)} async-done(((f32[768,3072]{1,0:T(8,128)}), f32[24,3072]{1,0:T(8,128)}) %reduce-scatter.26.cloned.1.call-update) | async-done | bytes 294928 | tf_op jit(solution)/shard_map/reduce_scatter | solution.py:402
  1874.8 141.5 %reduce-scatter.28.cloned.1.call-done = f32[96,768]{1,0:T(8,128)} async-done(((f32[3072,768]{1,0:T(8,128)}), f32[96,768]{1,0:T(8,128)}) %reduce-scatter.28.cloned.1.call-update) | async-done | bytes 294928 | tf_op jit(solution)/shard_map/reduce_scatter | solution.py:403
  2016.3 104.4 %reduce-scatter.30.cloned.1.call-done = f32[24,768]{1,0:T(8,128)} async-done(((f32[768,768]{1,0:T(8,128)}), f32[24,768]{1,0:T(8,128)}) %reduce-scatter.30.cloned.1.call-update) | async-done | bytes 73744
  (391 shorter events, 273.7 us)
Async XLA Ops:
  7.2 223.0 %all-gather.20.cloned.1.call-start = ((), (), s32[]{:S(2)}) async-start(), calls=%async_computation.10 | async-start | bytes 1216512 | tf_op jit(solution)/shard_map/all_gather | solution.py:149
  7.9 268.6 %all-gather.18.cloned.1.call-start = ((), (), s32[]{:S(2)}) async-start(), calls=%async_computation.9 | async-start | bytes 1966080 | tf_op jit(solution)/shard_map/all_gather | solution.py:177
  86.5 91.8 %copy-start.88 = (bf16[24]{0:T(256)(128)(2,1)S(1)}, bf16[24]{0:T(256)(128)(2,1)}, u32[]{:S(2)}) copy-start(bf16[24]{0:T(256)(128)(2,1)} %param.39) | copy-start | bytes 148
  86.5 92.1 %copy-start.89 = (bf16[24]{0:T(256)(128)(2,1)S(1)}, bf16[24]{0:T(256)(128)(2,1)}, u32[]{:S(2)}) copy-start(bf16[24]{0:T(256)(128)(2,1)} %param.40) | copy-start | bytes 148
  86.5 92.3 %copy-start.90 = (bf16[24]{0:T(256)(128)(2,1)S(1)}, bf16[24]{0:T(256)(128)(2,1)}, u32[]{:S(2)}) copy-start(bf16[24]{0:T(256)(128)(2,1)} %param.43) | copy-start | bytes 148
  86.5 130.3 %copy-start.83 = (u32[32]{0:T(128)S(1)}, u32[32]{0:T(128)}, u32[]{:S(2)}) copy-start(u32[32]{0:T(128)} %constant.312) | copy-start | bytes 388
  86.5 301.0 %all-gather.32.cloned.1.call-start = ((), (), s32[]{:S(2)}) async-start(), calls=%async_computation.24 | async-start | bytes 31850496 | tf_op jit(solution)/shard_map/all_gather | solution.py:21
  176.2 73.9 %copy-start.30 = (f32[576,64]{1,0:T(8,128)}, f32[576,64]{1,0:T(8,128)S(1)}, u32[]{:S(2)}) copy-start(f32[576,64]{1,0:T(8,128)S(1)} %gather_fusion.3) | copy-start | bytes 442372
  177.9 72.2 %copy-start.32 = (f32[576,64]{1,0:T(8,128)}, f32[576,64]{1,0:T(8,128)S(1)}, u32[]{:S(2)}) copy-start(f32[576,64]{1,0:T(8,128)S(1)} %gather_fusion.2) | copy-start | bytes 442372
  177.9 129.0 %copy-start.55 = (pred[576]{0:T(1024)(128)(4,1)}, pred[576]{0:T(1024)(128)(4,1)S(1)}, u32[]{:S(2)}) copy-start(pred[576]{0:T(1024)(128)(4,1)S(1)} %get-tuple-element.431) | copy-start | bytes 1732
  177.9 129.0 %copy-start.58 = (pred[576]{0:T(1024)(128)(4,1)}, pred[576]{0:T(1024)(128)(4,1)S(1)}, u32[]{:S(2)}) copy-start(pred[576]{0:T(1024)(128)(4,1)S(1)} %get-tuple-element.432) | copy-start | bytes 1732
  178.3 86.4 %copy-start.37 = (bf16[64,576]{1,0:T(8,128)(2,1)}, bf16[64,576]{1,0:T(8,128)(2,1)S(1)}, u32[]{:S(2)}) copy-start(bf16[64,576]{1,0:T(8,128)(2,1)S(1)} %copy.138) | copy-start | bytes 221188
  230.2 19.9 copy-start.51
  250.1 335.2 %reduce-scatter.14.cloned.1.call-start = ((), (), s32[]{:S(2)}) async-start(), calls=%async_computation.11 | async-start | bytes 3932160 | tf_op jit(solution)/shard_map/reduce_scatter | solution.py:209
  410.4 174.9 %copy-start.7 = (bf16[1,1,512,768]{3,2,1,0:T(8,128)(2,1)S(1)}, bf16[1,1,512,768]{3,2,1,0:T(8,128)(2,1)}, u32[]{:S(2)}) copy-start(bf16[1,1,512,768]{3,2,1,0:T(8,128)(2,1)} %param.30) | copy-start | bytes 2359300
  410.4 237.6 %all-gather.22.cloned.1.call-start = ((), (), s32[]{:S(2)}) async-start(), calls=%async_computation.12 | async-start | bytes 3649536 | tf_op jit(solution)/shard_map/all_gather | solution.py:152
  411.0 292.5 %all-gather.24.cloned.1.call-start = ((), (), s32[]{:S(2)}) async-start(), calls=%async_computation.13 | async-start | bytes 1216512 | tf_op jit(solution)/shard_map/all_gather | solution.py:153
  411.6 357.3 %all-gather.26.cloned.1.call-start = ((), (), s32[]{:S(2)}) async-start(), calls=%async_computation.14 | async-start | bytes 4866048 | tf_op jit(solution)/shard_map/all_gather | solution.py:155
  412.3 421.2 %all-gather.28.cloned.1.call-start = ((), (), s32[]{:S(2)}) async-start(), calls=%async_computation.15 | async-start | bytes 4866048 | tf_op jit(solution)/shard_map/all_gather | solution.py:156
  413.1 531.8 %all-gather.30.cloned.1.call-start = ((), (), s32[]{:S(2)}) async-start(), calls=%async_computation.16 | async-start | bytes 3932160 | tf_op jit(solution)/shard_map/all_gather | solution.py:318
  413.6 467.5 %copy-start.65 = (f32[768]{0:T(1024)}, f32[768]{0:T(1024)S(1)}, u32[]{:S(2)}) copy-start(f32[768]{0:T(1024)S(1)} %convert_element_type.313) | copy-start | bytes 9220
  414.4 238.1 %copy-start.70 = (f32[4,576]{1,0:T(4,128)}, f32[4,576]{1,0:T(4,128)S(1)}, u32[]{:S(2)}) copy-start(f32[4,576]{1,0:T(4,128)S(1)} %add_multiply_fusion) | copy-start | bytes 27652
  428.9 452.1 %copy-start.53 = (f32[512]{0:T(512)}, f32[512]{0:T(512)S(1)}, u32[]{:S(2)}) copy-start(f32[512]{0:T(512)S(1)} %convert_add_fusion.4) | copy-start | bytes 6148
  586.8 294.2 %copy-start.63 = (f32[512]{0:T(512)}, f32[512]{0:T(512)S(1)}, u32[]{:S(2)}) copy-start(f32[512]{0:T(512)S(1)} %broadcast_multiply_fusion.6) | copy-start | bytes 6148
  588.5 292.5 %copy-start.72 = (f32[512]{0:T(512)}, f32[512]{0:T(512)S(1)}, u32[]{:S(2)}) copy-start(f32[512]{0:T(512)S(1)} %add_rsqrt_fusion.1) | copy-start | bytes 6148
  661.1 42.4 %copy-start.11 = (bf16[512,768]{1,0:T(8,128)(2,1)S(1)}, bf16[512,768]{1,0:T(8,128)(2,1)}, u32[]{:S(2)}) copy-start(bf16[512,768]{1,0:T(8,128)(2,1)} %reduce-scatter.14.cloned.1.call-done) | copy-start | bytes 2359300
  705.9 139.9 %copy-start.5 = (f32[512,768]{1,0:T(8,128)}, f32[512,768]{1,0:T(8,128)S(1)}, u32[]{:S(2)}) copy-start(f32[512,768]{1,0:T(8,128)S(1)} %get-tuple-element.424) | copy-start | bytes 4718596
  706.0 139.9 %copy-start.46 = (f32[512]{0:T(512)}, f32[512]{0:T(512)S(1)}, u32[]{:S(2)}) copy-start(f32[512]{0:T(512)S(1)} %broadcast_multiply_fusion.5) | copy-start | bytes 6148
  706.3 139.6 %copy-start.48 = (f32[512]{0:T(512)}, f32[512]{0:T(512)S(1)}, u32[]{:S(2)}) copy-start(f32[512]{0:T(512)S(1)} %add_rsqrt_fusion) | copy-start | bytes 6148
  706.3 127.3 %copy-start.39 = (bf16[1,1,512,768]{3,2,1,0:T(8,128)(2,1)S(1)}, bf16[1,1,512,768]{3,2,1,0:T(8,128)(2,1)}, u32[]{:S(2)}) copy-start(bf16[1,1,512,768]{3,2,1,0:T(8,128)(2,1)} %param.31) | copy-start | bytes 2359300
  847.1 34.0 %copy-start.3 = (f32[512,768]{1,0:T(8,128)}, f32[512,768]{1,0:T(8,128)S(1)}, u32[]{:S(2)}) copy-start(f32[512,768]{1,0:T(8,128)S(1)} %multiply_add_fusion.1) | copy-start | bytes 4718596
  881.1 63.8 %copy-start.71 = (f32[4,576]{1,0:T(4,128)S(1)}, f32[4,576]{1,0:T(4,128)}, u32[]{:S(2)}) copy-start(f32[4,576]{1,0:T(4,128)} %copy-done.70) | copy-start | bytes 27652
  882.9 67.0 %copy-start.1 = (f32[512,768]{1,0:T(8,128)}, f32[512,768]{1,0:T(8,128)S(1)}, u32[]{:S(2)}) copy-start(f32[512,768]{1,0:T(8,128)S(1)} %get-tuple-element.405) | copy-start | bytes 4718596
  882.9 165.2 %reduce-scatter.16.cloned.1.call-start = ((), (), s32[]{:S(2)}) async-start(), calls=%async_computation.17 | async-start | bytes 1966080 | tf_op jit(solution)/shard_map/reduce_scatter | solution.py:363
  1014.0 173.5 %all-gather.34.cloned.1.call-start = ((), (), s32[]{:S(2)}) async-start(), calls=%async_computation.25 | async-start | bytes 31850496 | tf_op jit(solution)/shard_map/all_gather | solution.py:45
  1020.1 28.1 %copy-start.9 = (bf16[1,1,512,768]{3,2,1,0:T(8,128)(2,1)S(1)}, bf16[1,1,512,768]{3,2,1,0:T(8,128)(2,1)}, u32[]{:S(2)}) copy-start(bf16[1,1,512,768]{3,2,1,0:T(8,128)(2,1)} %param.30) | copy-start | bytes 2359300
  1020.1 324.0 %reduce-scatter.18.cloned.1.call-start = ((), (), s32[]{:S(2)}) async-start(), calls=%async_computation.18 | async-start | bytes 61440 | tf_op jit(solution)/shard_map/reduce_scatter | solution.py:366
  1325.6 18.5 copy-start.10
  1325.6 51.0 %reduce-scatter.20.cloned.1.call-start = ((), (), s32[]{:S(2)}) async-start(), calls=%async_computation.19 | async-start | bytes 122880 | tf_op jit(solution)/shard_map/reduce_scatter | solution.py:369
  1333.8 170.5 %all-reduce.17.cloned.1.call-start = ((), (), s32[]{:S(2)}) async-start(), calls=%async_computation.27 | async-start | bytes 4718592
  1346.3 262.3 %reduce-scatter.24.cloned.1.call-start = ((), (), s32[]{:S(2)}) async-start(), calls=%async_computation.21 | async-start | bytes 2433024 | tf_op jit(solution)/shard_map/reduce_scatter | solution.py:400
  1349.8 383.7 %reduce-scatter.22.cloned.1.call-start = ((), (), s32[]{:S(2)}) async-start(), calls=%async_computation.20 | async-start | bytes 7299072 | tf_op jit(solution)/shard_map/reduce_scatter | solution.py:399
  1356.9 517.8 %reduce-scatter.26.cloned.1.call-start = ((), (), s32[]{:S(2)}) async-start(), calls=%async_computation.22 | async-start | bytes 9732096 | tf_op jit(solution)/shard_map/reduce_scatter | solution.py:402
  1365.6 650.7 %reduce-scatter.28.cloned.1.call-start = ((), (), s32[]{:S(2)}) async-start(), calls=%async_computation.23 | async-start | bytes 9732096 | tf_op jit(solution)/shard_map/reduce_scatter | solution.py:403
  1376.3 744.4 %reduce-scatter.30.cloned.1.call-start = ((), (), s32[]{:S(2)}) async-start(), calls=%async_computation.26 | async-start | bytes 2433024
  1392.2 53.1 %copy-start.22 = (bf16[768,384]{1,0:T(8,128)(2,1)S(1)}, bf16[768,384]{1,0:T(8,128)(2,1)}, u32[]{:S(2)}) copy-start(bf16[768,384]{1,0:T(8,128)(2,1)} %copy-done.21) | copy-start | bytes 1769476
  1392.2 53.0 %copy-start.50 = (bf16[16,384]{1,0:T(8,128)(2,1)S(1)}, bf16[16,384]{1,0:T(8,128)(2,1)}, u32[]{:S(2)}) copy-start(bf16[16,384]{1,0:T(8,128)(2,1)} %reduce-scatter.18.cloned.1.call-done) | copy-start | bytes 36868
  1392.2 53.3 %copy-start.45 = (bf16[16,768]{1,0:T(8,128)(2,1)S(1)}, bf16[16,768]{1,0:T(8,128)(2,1)}, u32[]{:S(2)}) copy-start(bf16[16,768]{1,0:T(8,128)(2,1)} %reduce-scatter.20.cloned.1.call-done) | copy-start | bytes 73732
  (67 other events, 420.1 us)
Sparse Core Ops, SparseCore 0:
  10.8 57.1 all-gather.19
  86.6 38.2 all-gather.17
  250.2 137.2 all-gather.31
  410.5 174.6 reduce-scatter.13
  587.9 60.0 all-gather.21
  650.7 52.7 all-gather.23
  706.3 62.5 all-gather.25
  771.6 61.8 all-gather.27
  883.0 61.8 all-gather.29
  1014.1 34.0 reduce-scatter.15
  1050.1 137.3 all-gather.33
  1325.7 18.3 reduce-scatter.17
  1347.0 17.5 reduce-scatter.19
  1370.1 134.1 all-reduce.16
  1510.0 98.5 reduce-scatter.23
  1614.7 118.6 reduce-scatter.21
  1739.7 134.9 reduce-scatter.25
  1881.1 135.1 reduce-scatter.27
  2022.1 98.5 reduce-scatter.29
where the time goes:
time: 2140 us; the launch traced here: 2130 us
  waiting for transfers between devices  1330 us (62%)
  blocking collectives  330 us (15%)
  other arithmetic  171 us (8%)
  matrix products  148 us (7%)
  local copies, waits for them, and re-layouts  129 us (6%)
    unnamed x21, waiting for transfers between devices  164 us
    reduce_scatter x1, waiting for transfers between devices, body(): lax.psum_scatter(part_num.astype(jnp.bfloat16), 'narrow', scatter_dimensi...  156 us
    reduce_scatter x1, waiting for transfers between devices, body(): lax.psum_scatter(grad_reduce, ('dp', 'narrow'), scatter_dimension=0, tile...  141 us
    reduce_scatter x1, waiting for transfers between devices, body(): lax.psum_scatter(grad_expand, ('dp', 'narrow'), scatter_dimension=0, tile...  141 us
    all_gather x1, waiting for transfers between devices, entering(): lax.all_gather(a.astype(kind), axis)  137 us
    reduce_scatter x1, waiting for transfers between devices, body(): lax.psum_scatter(grad_mixing, ('dp', 'narrow'), scatter_dimension=0, tile...  125 us
    unnamed x6, blocking collectives  121 us
    reduce_scatter x1, waiting for transfers between devices, body(): lax.psum_scatter(grad_output, ('dp', 'narrow'), scatter_dimension=0, tile...  101 us
  transfers between devices with their start and end apart: 19, of which 16 were waited for; matrix products, arithmetic and copies ran while one was open for 8% of the time, Pallas kernels for 0%

commit v1 on v0

--- a/solution.py
+++ b/solution.py
@@ -6,6 +6,7 @@
 HEADS = 12
 HD = 64
 MEM = 16
+ORDER = 3
 
 
 exact_mode = lax.Precision.HIGHEST
@@ -15,53 +16,6 @@
 float_kind = jnp.float32
 
 
-def carried_in(value, axis, join, neutral):
-    place = lax.axis_index(axis)
-    gathered = jax.tree.map(
-        lambda a, kind: lax.all_gather(a.astype(kind), axis),
-        value,
-        (jnp.bfloat16, jnp.bfloat16, jnp.bfloat16),
-    )
-    state = jax.tree.map(lambda a, e: jnp.zeros_like(a) + jnp.asarray(e, a.dtype), value, neutral)
-
-    def carried_one(turn, state):
-        return join(
-            state,
-            jax.tree.map(
-                lambda a, own: lax.dynamic_index_in_dim(a, turn, 0, False).astype(own.dtype),
-                gathered,
-                value,
-            ),
-        )
-
-    return lax.fori_loop(0, place, carried_one, state)
-
-
-def entering(value, axis, join, neutral):
-    count = lax.axis_size(axis)
-    place = lax.axis_index(axis)
-    ahead = count - 1 - place
-    gathered = jax.tree.map(
-        lambda a, kind: lax.all_gather(a.astype(kind), axis),
-        value,
-        jax.tree.map(lambda a: jnp.bfloat16 if a.dtype == jnp.float32 else a.dtype, value),
-    )
-    state = jax.tree.map(lambda a, e: jnp.zeros_like(a) + jnp.asarray(e, a.dtype), value, neutral)
-
-    def entering_one(turn, state):
-        source = count - 1 - turn
-        return join(
-            state,
-            jax.tree.map(
-                lambda a, own: lax.dynamic_index_in_dim(a, source, 0, False).astype(own.dtype),
-                gathered,
-                value,
-            ),
-        )
-
-    return lax.fori_loop(0, ahead, entering_one, state)
-
-
 def matmul(left, right):
     return jnp.dot(left, right, preferred_element_type=float_kind)
 
@@ -74,18 +28,28 @@
     return jnp.concatenate([jax.nn.relu(inputs), jax.nn.relu(-inputs)], axis=-1)
 
 
-def column_features(inputs, first_idx, second_idx):
+def features(inputs):
     halves = halves_of(inputs)
-    return jnp.take(halves, first_idx, axis=-1) * jnp.take(halves, second_idx, axis=-1)
-
-
-def own_columns(key_width, col_count):
-    first_col = lax.axis_index("narrow") * col_count
-    columns = first_col + jnp.arange(col_count, dtype=jnp.int32)
-    within = columns % (2 * key_width)
-    block_num = columns // (2 * key_width)
-    partner = (within - block_num - 1) % (2 * key_width)
-    return (within, partner)
+    return jnp.concatenate(
+        [halves * jnp.roll(halves, shift, axis=-1) for shift in range(1, ORDER + 1)], axis=-1
+    )
+
+
+def features_back(inputs, grad):
+    key_width = inputs.shape[-1]
+    halves = halves_of(inputs)
+    total = jnp.zeros_like(halves)
+    for shift in range(1, ORDER + 1):
+        part = grad[:, (shift - 1) * 2 * key_width : shift * 2 * key_width]
+        total = total + part * jnp.roll(halves, shift, axis=-1)
+        total = total + jnp.roll(part * halves, -shift, axis=-1)
+    return jnp.where(inputs > 0, total[:, :key_width], 0.0) - jnp.where(
+        inputs < 0, total[:, key_width:], 0.0
+    )
+
+
+def exact(left, right):
+    return jnp.dot(left, right, precision=exact_mode)
 
 
 def norm_forward(inputs, gain):
@@ -104,16 +68,6 @@
         - unit * jnp.mean(grad_unit * unit, axis=-1, keepdims=True)
     )
     return (grad_in, grad_gain)
-
-
-def chain(earlier, later):
-    keep_early, memory_early, normal_early = earlier
-    keep_late, memory_late, normalizer_final = later
-    return (
-        keep_early * keep_late,
-        memory_early * keep_late[:, None, None] + memory_late,
-        normal_early * keep_late[:, None] + normalizer_final,
-    )
 
 
 def block_scores(query_blk, key_seg, row_start):
@@ -161,7 +115,6 @@
     row_count = seg_count * seg_len
     key_width = query_w.shape[1]
     stream_count = memory_state.shape[0]
-    col_count = memory_state.shape[2]
     gain_one_f = gain_one.astype(float_kind)
     gain_two_f = gain_two.astype(float_kind)
     tok_rows = tokens.reshape(row_count, width)
@@ -171,48 +124,55 @@
     write_vals = matmul(memory_rows, value_w).astype(bf_type)
     gate_prob = jax.nn.sigmoid(matmul(memory_rows, gate_w))
     gate_low = gate_prob.astype(bf_type)
-    first_idx, second_idx = own_columns(key_width, col_count)
-    keep_flag = 1.0 - resets[:, 0].astype(float_kind)
-    all_query, all_keys, all_vals, all_gates = (
-        lax.all_gather(mem_query, "narrow", axis=0, tiled=True),
-        lax.all_gather(write_keys, "narrow", axis=0, tiled=True),
-        lax.all_gather(write_vals, "narrow", axis=0, tiled=True),
-        lax.all_gather(gate_low, "narrow", axis=0, tiled=True),
-    )
-    key_feat = rounded(column_features(all_keys.astype(float_kind), first_idx, second_idx)).reshape(
-        stream_count, MEM, col_count
-    )
-    gates_f = all_gates.astype(float_kind).reshape(stream_count, MEM, 1)
-    vals_f = all_vals.astype(float_kind).reshape(stream_count, MEM, width)
-    scaled_vals = vals_f * gates_f
-    delta = jnp.einsum("smd,smc->sdc", scaled_vals, key_feat, precision=exact_mode)
-    delta_norm = jnp.sum(key_feat, axis=1)
-    identity = (jnp.ones_like(keep_flag), jnp.zeros_like(delta), jnp.zeros_like(delta_norm))
-    prod_keep, acc_memory, acc_normal = carried_in(
-        (keep_flag, delta, delta_norm), "dp", chain, identity
-    )
-    memory_now = keep_flag[:, None, None] * (prod_keep[:, None, None] * memory_state + acc_memory)
-    normal_now = keep_flag[:, None] * (prod_keep[:, None] * normalizer + acc_normal)
-    query_features = (
-        column_features(all_query.astype(float_kind), first_idx, second_idx)
-        .astype(bf_type)
-        .reshape(stream_count, seg_len, col_count)
-    )
-    memory_reduced_precision = memory_now.astype(bf_type)
-    part_num = jnp.einsum(
-        "nuz,nwz->nuw", query_features, memory_reduced_precision, preferred_element_type=float_kind
-    ).reshape(stream_count * seg_len, width)
-    part_den = jnp.einsum(
-        "slc,sc->sl", query_features.astype(float_kind), normal_now, precision=exact_mode
-    ).reshape(stream_count * seg_len)
-    numerator, den_sum = (
-        lax.psum_scatter(
-            part_num.astype(jnp.bfloat16), "narrow", scatter_dimension=0, tiled=True
-        ).astype(jnp.float32),
-        lax.psum_scatter(
-            part_den.astype(jnp.bfloat16), "narrow", scatter_dimension=0, tiled=True
-        ).astype(jnp.float32),
-    )
+    place = lax.axis_index("dp")
+    places = lax.axis_size("dp")
+    stream = lax.axis_index("narrow")
+    keep_flag = 1.0 - resets.astype(float_kind)
+    own_keep = lax.dynamic_index_in_dim(keep_flag[:, 0], stream, 0, False)
+    packed = jnp.concatenate(
+        [
+            write_keys,
+            write_vals,
+            jnp.broadcast_to(gate_low[:, None], (MEM, 64)),
+            jnp.broadcast_to(own_keep.astype(bf_type), (MEM, 64)),
+        ],
+        axis=1,
+    )
+    all_rows = lax.all_gather(packed, "dp", axis=0, tiled=True).astype(float_kind)
+    all_keys = all_rows[:, :key_width]
+    all_vals = all_rows[:, key_width : key_width + width]
+    all_gates = all_rows[:, key_width + width : key_width + width + 1]
+    keeps = all_rows[::MEM, key_width + width + 64]
+    index = jnp.arange(places)
+    linked = jnp.prod(
+        jnp.where(
+            (index[None, :] > index[:, None]) & (index[None, :] <= place), keeps[None, :], 1.0
+        ),
+        axis=1,
+    ) * (index < place)
+    start_keep = jnp.prod(jnp.where(index <= place, keeps, 1.0))
+    row_link = jnp.repeat(linked, MEM)[None, :]
+    key_feat = features(all_keys).astype(bf_type)
+    scaled_vals = all_vals * all_gates
+    memory_parts = lax.all_to_all(memory_state.astype(bf_type), "narrow", 0, 0, tiled=True)
+    memory_own = jnp.concatenate(
+        [memory_parts[i] for i in range(stream_count)], axis=-1
+    )
+    normal_all = lax.all_gather(normalizer, "narrow", axis=1, tiled=True)
+    normal_own = lax.dynamic_index_in_dim(normal_all, stream, 0, False)
+    query_features = features(mem_query.astype(float_kind)).astype(bf_type)
+    row_scores = (
+        lax.dot_general(
+            query_features, key_feat, (((1,), (1,)), ((), ())), preferred_element_type=float_kind
+        )
+        * row_link
+    )
+    numerator = start_keep * lax.dot_general(
+        query_features, memory_own, (((1,), (1,)), ((), ())), preferred_element_type=float_kind
+    ) + exact(row_scores, scaled_vals)
+    den_sum = start_keep * jnp.sum(
+        query_features.astype(float_kind) * normal_own[None, :], axis=1
+    ) + jnp.sum(row_scores, axis=1)
     den_total = 1.0 + den_sum
     first_res = tok_rows.astype(float_kind) + numerator / den_total[:, None]
     normed_one, unit_one, inv_one = norm_forward(first_res, gain_one_f)
@@ -314,65 +274,24 @@
     grad_first = grad_second + grad_in_one
     grad_num = (grad_first / den_total[:, None]).astype(bf_type)
     grad_den = (-jnp.sum(grad_first * numerator, axis=-1) / (den_total * den_total)).astype(bf_type)
-    all_gnum, all_gden = (
-        lax.all_gather(grad_num, "narrow", axis=0, tiled=True),
-        lax.all_gather(grad_den, "narrow", axis=0, tiled=True),
-    )
-    gate_numerator_segment = all_gnum.reshape(stream_count, seg_len, width)
-    gden_seg = all_gden.astype(float_kind).reshape(stream_count, seg_len)
-    grad_feat = (
-        jnp.einsum(
-            "ait,ato->aio",
-            gate_numerator_segment,
-            memory_reduced_precision,
-            preferred_element_type=float_kind,
-        )
-        + gden_seg[:, :, None] * normal_now[:, None, :]
-    )
-    memory_gradient = jnp.einsum(
-        "nkj,nkg->njg", gate_numerator_segment, query_features, preferred_element_type=float_kind
-    )
-    grad_normal = jnp.einsum(
-        "sl,slc->sc", gden_seg, query_features.astype(float_kind), precision=exact_mode
-    )
-    unused, feat_pull = jax.vjp(
-        lambda inputs: column_features(inputs, first_idx, second_idx), all_query.astype(float_kind)
-    )
-    query_part = feat_pull(grad_feat.reshape(stream_count * seg_len, col_count))[0]
-    backward_entries = (
-        keep_flag,
-        keep_flag[:, None, None] * memory_gradient,
-        keep_flag[:, None] * grad_normal,
-    )
-    unused_keep, grad_delta, grad_delta_norm = entering(backward_entries, "dp", chain, identity)
-    live = (lax.axis_index("dp") >= lax.axis_size("dp") - truncation).astype(float_kind)
-    grad_delta = grad_delta * live[:, None, None]
-    grad_delta_norm = grad_delta_norm * live[:, None]
-    grad_scaled = jnp.einsum("sdc,smc->smd", grad_delta, key_feat, precision=exact_mode)
-    vals_part = (grad_scaled * gates_f).reshape(stream_count * MEM, width)
-    gates_part = jnp.sum(grad_scaled * vals_f, axis=-1).reshape(stream_count * MEM)
-    grad_kfeat = (
-        jnp.einsum("smd,sdc->smc", scaled_vals, grad_delta, precision=exact_mode)
-        + grad_delta_norm[:, None, :]
-    )
-    unused, key_pull = jax.vjp(
-        lambda inputs: column_features(inputs, first_idx, second_idx), all_keys.astype(float_kind)
-    )
-    keys_part = key_pull(grad_kfeat.reshape(stream_count * MEM, col_count))[0]
-    grad_mq, grad_wk, grad_wv, grad_gate = (
-        lax.psum_scatter(
-            query_part.astype(jnp.bfloat16), "narrow", scatter_dimension=0, tiled=True
-        ).astype(jnp.float32),
-        lax.psum_scatter(
-            keys_part.astype(jnp.bfloat16), "narrow", scatter_dimension=0, tiled=True
-        ).astype(jnp.float32),
-        lax.psum_scatter(
-            vals_part.astype(jnp.bfloat16), "narrow", scatter_dimension=0, tiled=True
-        ).astype(jnp.float32),
-        lax.psum_scatter(
-            gates_part.astype(jnp.bfloat16), "narrow", scatter_dimension=0, tiled=True
-        ).astype(jnp.float32),
-    )
+    grad_num_f = grad_num.astype(float_kind)
+    grad_den_f = grad_den.astype(float_kind)[:, None]
+    grad_scores_mem = (exact(grad_num_f, scaled_vals.T) + grad_den_f) * row_link
+    grad_feat = start_keep * (
+        matmul(grad_num, memory_own) + grad_den_f * normal_own[None, :]
+    ) + exact(grad_scores_mem, key_feat.astype(float_kind))
+    grad_mq = features_back(mem_query.astype(float_kind), grad_feat)
+    grad_key_feat = exact(grad_scores_mem.T, query_features.astype(float_kind))
+    grad_rows = jnp.concatenate(
+        [features_back(all_keys, grad_key_feat), exact(row_scores.T, grad_num_f)], axis=1
+    )
+    live = (place >= places - lax.dynamic_index_in_dim(truncation, stream, 0, False)).astype(
+        float_kind
+    )
+    own_rows = lax.psum_scatter(grad_rows, "dp", scatter_dimension=0, tiled=True) * live
+    grad_wk = own_rows[:, :key_width]
+    grad_wv = own_rows[:, key_width:] * gate_low.astype(float_kind)[:, None]
+    grad_gate = jnp.sum(own_rows[:, key_width:] * write_vals.astype(float_kind), axis=1)
     grad_mq_low = grad_mq.astype(bf_type)
     grad_wk_low = grad_wk.astype(bf_type)
     grad_wv_low = grad_wv.astype(bf_type)

time: 2140 us -> 1260 us (0.59)
  waiting for transfers between devices: 1330 us -> 682 us
  other arithmetic: 171 us -> 39.9 us
  local copies, waits for them, and re-layouts: 129 us -> 52.8 us
    all_gather x4 -> x0, waiting for transfers between devices: 256 us -> none  [the longest x1 137 us: entering(): lax.all_gather(a.astype(kind), axis)]
    reduce_scatter x4 -> x1, waiting for transfers between devices: 183 us -> 24.9 us  [body(): lax.psum_scatter(grad_rows, 'dp', scatter_dimension=0, tiled=True) * live]
    all_gather x1, blocking collectives: 75.2 us -> 150 us  [body(): lax.all_gather(query_weight, ('dp', 'narrow'), axis=0, tiled=True)]
    all_gather x1, waiting for transfers between devices: 62.5 us -> 0.01 us  [body(): lax.all_gather(expand_weight, ('dp', 'narrow'), axis=0, tiled=True)]
    all_gather x1, waiting for transfers between devices: 59.5 us -> 0.01 us  [body(): lax.all_gather(mixing_weight, ('dp', 'narrow'), axis=0, tiled=True)]
    all_gather x1, waiting for transfers between devices: 57.7 us -> 0.01 us  [body(): lax.all_gather(reduce_weight, ('dp', 'narrow'), axis=0, tiled=True)]
    add x14 -> x2, other arithmetic: 63.4 us -> 5.72 us  [features_back(): total = total + jnp.roll(part * halves, -shift, axis=-1)]
    scatter-add x4 -> x0, other arithmetic: 54.4 us -> none  [the longest x2 27.3 us: column_features(): jnp.take(halves, second_idx, axis=-1)]
  transfers between devices with their start and end apart: 19 -> 13, of which waited for: 16 -> 7; matrix products, arithmetic and copies ran while one was open for 8% -> 10% of each run, Pallas kernels for 0% -> 0%
where the time goes in v1:
time: 1260 us; the launch traced here: 1250 us
  waiting for transfers between devices  682 us (54%)
  blocking collectives  322 us (26%)
  matrix products  127 us (10%)
  local copies, waits for them, and re-layouts  52.8 us (4%)
  other arithmetic  39.9 us (3%)
  between operations  16.6 us (1%)
    all_gather x1, blocking collectives, body(): lax.all_gather(query_weight, ('dp', 'narrow'), axis=0, tiled=True)  150 us
    unnamed x14, waiting for transfers between devices  148 us
    reduce_scatter x1, waiting for transfers between devices, body(): lax.psum_scatter(grad_expand, ('dp', 'narrow'), scatter_dimension=0, tile...  142 us
    reduce_scatter x1, waiting for transfers between devices, body(): lax.psum_scatter(grad_reduce, ('dp', 'narrow'), scatter_dimension=0, tile...  142 us
    reduce_scatter x1, waiting for transfers between devices, body(): lax.psum_scatter(grad_mixing, ('dp', 'narrow'), scatter_dimension=0, tile...  125 us
    reduce_scatter x1, waiting for transfers between devices, body(): lax.psum_scatter(grad_output, ('dp', 'narrow'), scatter_dimension=0, tile...  101 us
    dot_general x23, matrix products, matmul(): return jnp.dot(left, right, preferred_element_type=float_kind)  84.8 us
    unnamed x2, blocking collectives  76.6 us
  transfers between devices with their start and end apart: 13, of which 7 were waited for; matrix products, arithmetic and copies ran while one was open for 10% of the time, Pallas kernels for 0%

profile of v1, /device:TPU:0, one launch (start us, length us, event | category | flops | bytes accessed | tf_op | source)
XLA Modules:
  0.0 1248.1 jit_solution(7343517955284938279)
XLA Ops:
  10.0 5.2 convert_element_type.169
  15.1 6.5 all-to-all-start
  22.3 149.9 %all_gather.40 = bf16[768,384]{1,0:T(8,128)(2,1)S(1)} all-gather(bf16[24,384]{1,0:T(8,128)(2,1)S(1)} %copy-done.102), channel_id=1, replica_groups=mesh['dp'=8,'narrow'=4] {'dp','narrow'}, dimensions={0}, use_global_device_ids=true | all-gather | bytes 608256 | tf_op jit(solution)/shard_map/all_gather | solution.py:101
  176.9 36.9 %all-reduce.10 = (bf16[768]{0:T(1024)(128)(2,1)S(1)}, bf16[768]{0:T(1024)(128)(2,1)S(1)}, bf16[768]{0:T(1024)(128)(2,1)S(1)}) all-reduce(bf16[768]{0:T(1024)(128)(2,1)S(1)} %dynamic-update-slice.4, bf16[768]{0:T(1024)(128)(2,1)S(1)} %dynamic-update-slice.5, ...), channel_id=1, replica_groups=mesh['dp'=8,'narrow'=4] {'dp','narrow'}, use_global_device_ids=true, to_apply=%add | all-reduce | flops 2304 | bytes 9216
  214.5 13.9 %all-gather = f32[4,576,4]{1,2,0:T(4,128)S(1)} all-gather(f32[1,576,4]{1,2,0:T(4,128)S(1)} %bitcast.151), channel_id=1, replica_groups=mesh['dp'=8,'narrow'=4] {'narrow'}, dimensions={0}, use_global_device_ids=true | all-gather | bytes 46080 | tf_op jit(solution)/shard_map/all_gather | solution.py:161
  232.5 72.0 %all_gather.36 = bf16[768,384]{1,0:T(8,128)(2,1)S(1)} all-gather(bf16[24,384]{1,0:T(8,128)(2,1)S(1)} %copy-done.103), channel_id=1, replica_groups=mesh['dp'=8,'narrow'=4] {'dp','narrow'}, dimensions={0}, use_global_device_ids=true | all-gather | bytes 608256 | tf_op jit(solution)/shard_map/all_gather | solution.py:102
  305.6 4.4 multiply_reduce_fusion.1
  312.4 9.9 all_gather.39
  330.4 2.4 slice_bitcast_fusion.3
  333.0 2.1 fusion.49
  335.4 3.5 fusion.93
  340.0 4.1 convolution_convert_fusion
  348.7 2.6 copy.77
  351.3 3.0 fusion.14
  354.4 4.3 fusion
  359.4 4.4 fusion.25
  363.8 2.9 fusion.97
  368.2 7.1 fusion.91
  375.3 8.9 fusion.8
  384.3 3.5 multiply_reduce_fusion.2
  389.5 1.7 convolution_convert_fusion.1
  391.3 2.3 copy.81
  393.6 9.0 fusion.22
  402.6 9.6 multiply_reduce_fusion
  412.3 7.3 multiply_convert_fusion
  419.6 2.0 multiply_convert_fusion.2
  424.8 3.1 multiply_reduce_fusion.3
  432.1 2.9 fusion.13
  435.0 2.4 fusion.92
  438.6 2.1 convolution_add_fusion
  449.5 5.3 fusion.21
  457.4 24.9 %reduce-scatter.11.cloned.1.call-done = f32[16,1152]{1,0:T(8,128)} async-done(((f32[128,1152]{1,0:T(8,128)}), f32[16,1152]{1,0:T(8,128)}) %reduce-scatter.11.cloned.1.call-update) | async-done | bytes 73744 | tf_op jit(solution)/shard_map/reduce_scatter | solution.py:291
  483.9 2.1 convolution_bitcast_fusion.1
  486.1 3.3 fusion.57
  490.9 2.7 convolution_bitcast_fusion
  493.6 3.1 copy.102
  498.1 6.9 fusion.36
  506.2 9.8 fusion.41
  516.6 7.3 fusion.90
  529.5 8.9 fusion.26
  539.3 39.7 %all-reduce.8 = (f32[768]{0:T(1024)S(1)}, f32[768]{0:T(1024)S(1)}, f32[768]{0:T(1024)S(1)}) all-reduce(f32[768]{0:T(1024)S(1)} %convolution_reduce_fusion, f32[768]{0:T(1024)S(1)} %copy-done.117, f32[768]{0:T(1024)S(1)} %copy-done.116), channel_id=6, replica_groups=mesh['dp'=8,'narrow'=4] {'dp','narrow'}, use_global_device_ids=true, to_apply=%region_21.22.clone | all-reduce | flops 2304 | bytes 18432
  581.0 2.4 fusion.31
  583.4 40.6 %all-reduce.13.cloned.1.call-done = (f32[768,384]{0,1:T(8,128)}, f32[768,384]{0,1:T(8,128)}) async-done(((f32[768,384]{0,1:T(8,128)}, f32[768,384]{0,1:T(8,128)}), (f32[768,384]{0,1:T(8,128)}, f32[768,384]{0,1:T(8,128)})) %all-reduce.13.cloned.1.call-update) | async-done | bytes 2359312
  627.6 100.8 %reduce-scatter.15.cloned.1.call-done = f32[24,768]{1,0:T(8,128)} async-done(((f32[768,768]{1,0:T(8,128)}), f32[24,768]{1,0:T(8,128)}) %reduce-scatter.15.cloned.1.call-update) | async-done | bytes 73744 | tf_op jit(solution)/shard_map/reduce_scatter | solution.py:319
  728.4 104.5 %reduce-scatter.21.cloned.1.call-done = f32[24,768]{1,0:T(8,128)} async-done(((f32[768,768]{1,0:T(8,128)}), f32[24,768]{1,0:T(8,128)}) %reduce-scatter.21.cloned.1.call-update) | async-done | bytes 73744
  832.9 124.7 %reduce-scatter.13.cloned.1.call-done = f32[24,2304]{1,0:T(8,128)} async-done(((f32[768,2304]{1,0:T(8,128)}), f32[24,2304]{1,0:T(8,128)}) %reduce-scatter.13.cloned.1.call-update) | async-done | bytes 221200 | tf_op jit(solution)/shard_map/reduce_scatter | solution.py:318
  957.6 141.7 %reduce-scatter.19.cloned.1.call-done = f32[96,768]{1,0:T(8,128)} async-done(((f32[3072,768]{1,0:T(8,128)}), f32[96,768]{1,0:T(8,128)}) %reduce-scatter.19.cloned.1.call-update) | async-done | bytes 294928 | tf_op jit(solution)/shard_map/reduce_scatter | solution.py:322
  1099.3 141.8 %reduce-scatter.17.cloned.1.call-done = f32[24,3072]{1,0:T(8,128)} async-done(((f32[768,3072]{1,0:T(8,128)}), f32[24,3072]{1,0:T(8,128)}) %reduce-scatter.17.cloned.1.call-update) | async-done | bytes 294928 | tf_op jit(solution)/shard_map/reduce_scatter | solution.py:321
  (403 shorter events, 71.4 us)
Async XLA Ops:
  7.2 302.8 %all-gather.7.cloned.1.call-start = ((), (), s32[]{:S(2)}) async-start(), calls=%async_computation.7 | async-start | bytes 1216512 | tf_op jit(solution)/shard_map/all_gather | solution.py:103
  7.9 332.1 %all-gather.9.cloned.1.call-start = ((), (), s32[]{:S(2)}) async-start(), calls=%async_computation.8 | async-start | bytes 3649536 | tf_op jit(solution)/shard_map/all_gather | solution.py:106
  8.7 355.1 %all-gather.11.cloned.1.call-start = ((), (), s32[]{:S(2)}) async-start(), calls=%async_computation.9 | async-start | bytes 1216512 | tf_op jit(solution)/shard_map/all_gather | solution.py:107
  9.4 358.8 %all-gather.13.cloned.1.call-start = ((), (), s32[]{:S(2)}) async-start(), calls=%async_computation.10 | async-start | bytes 4866048 | tf_op jit(solution)/shard_map/all_gather | solution.py:109
  15.1 7.2 copy-start.102
  15.1 157.9 %copy-start.24 = (bf16[1,1,512,768]{3,2,1,0:T(8,128)(2,1)S(1)}, bf16[1,1,512,768]{3,2,1,0:T(8,128)(2,1)}, u32[]{:S(2)}) copy-start(bf16[1,1,512,768]{3,2,1,0:T(8,128)(2,1)} %param.18) | copy-start | bytes 2359300
  15.1 315.2 %all-to-all-start = ((bf16[4,768,576]{1,2,0:T(8,128)(2,1)}), bf16[4,768,576]{1,2,0:T(8,128)(2,1)}, u32[]{:S(2)}, u32[]{:S(2)}) async-start(bf16[4,768,576]{1,2,0:T(8,128)(2,1)} %convert_element_type.169), calls=%async_computation | async-start | bytes 7077888 | tf_op jit(solution)/shard_map/all_to_all | solution.py:157
  21.6 152.8 %copy-start.125 = (s32[4]{0:T(128)S(1)}, s32[4]{0:T(128)}, u32[]{:S(2)}) copy-start(s32[4]{0:T(128)} %param.21) | copy-start | bytes 52
  21.6 154.0 %copy-start.126 = (s32[4,1]{0,1:T(1,128)S(1)}, s32[4,1]{0,1:T(1,128)}, u32[]{:S(2)}) copy-start(s32[4,1]{0,1:T(1,128)} %param.20) | copy-start | bytes 52
  21.6 154.7 %copy-start.127 = (bf16[24]{0:T(256)(128)(2,1)S(1)}, bf16[24]{0:T(256)(128)(2,1)}, u32[]{:S(2)}) copy-start(bf16[24]{0:T(256)(128)(2,1)} %param.28) | copy-start | bytes 148
  21.6 154.9 %copy-start.128 = (bf16[24]{0:T(256)(128)(2,1)S(1)}, bf16[24]{0:T(256)(128)(2,1)}, u32[]{:S(2)}) copy-start(bf16[24]{0:T(256)(128)(2,1)} %param.27) | copy-start | bytes 148
  21.6 155.1 %copy-start.129 = (bf16[24]{0:T(256)(128)(2,1)S(1)}, bf16[24]{0:T(256)(128)(2,1)}, u32[]{:S(2)}) copy-start(bf16[24]{0:T(256)(128)(2,1)} %param.31) | copy-start | bytes 148
  21.6 192.8 %copy-start.108 = (f32[4,576]{1,0:T(4,128)S(1)}, f32[4,576]{1,0:T(4,128)}, u32[]{:S(2)}) copy-start(f32[4,576]{1,0:T(4,128)} %param.23) | copy-start | bytes 27652
  21.7 353.7 %all-gather.15.cloned.1.call-start = ((), (), s32[]{:S(2)}) async-start(), calls=%async_computation.11 | async-start | bytes 4866048 | tf_op jit(solution)/shard_map/all_gather | solution.py:110
  22.3 460.1 %reduce-scatter.11.cloned.1.call-start = ((), (), s32[]{:S(2)}) async-start(), calls=%async_computation.12 | async-start | bytes 663552 | tf_op jit(solution)/shard_map/reduce_scatter | solution.py:291
  174.4 55.4 %copy-start.97 = (f32[512,1]{0,1:T(1,128)}, f32[512,1]{0,1:T(1,128)S(1)}, u32[]{:S(2)}) copy-start(f32[512,1]{0,1:T(1,128)S(1)} %slice.264) | copy-start | bytes 6148
  174.4 55.4 %copy-start.95 = (f32[512,2]{0,1:T(2,128)}, f32[512,2]{0,1:T(2,128)S(1)}, u32[]{:S(2)}) copy-start(f32[512,2]{0,1:T(2,128)S(1)} %slice.267) | copy-start | bytes 12292
  228.5 77.0 %copy-start.93 = (f32[2304]{0:T(1024)}, f32[2304]{0:T(1024)S(1)}, u32[]{:S(2)}) copy-start(f32[2304]{0:T(1024)S(1)} %dynamic-slice_reduce_fusion) | copy-start | bytes 27652
  231.8 73.8 %copy-start.39 = (bf16[512,768]{0,1:T(8,128)(2,1)}, bf16[512,768]{0,1:T(8,128)(2,1)S(1)}, u32[]{:S(2)}) copy-start(bf16[512,768]{0,1:T(8,128)(2,1)S(1)} %get-tuple-element.148) | copy-start | bytes 2359300
  231.8 73.8 %copy-start.43 = (bf16[512,768]{0,1:T(8,128)(2,1)}, bf16[512,768]{0,1:T(8,128)(2,1)S(1)}, u32[]{:S(2)}) copy-start(bf16[512,768]{0,1:T(8,128)(2,1)S(1)} %get-tuple-element.149) | copy-start | bytes 2359300
  231.8 73.8 %copy-start.47 = (bf16[512,768]{0,1:T(8,128)(2,1)}, bf16[512,768]{0,1:T(8,128)(2,1)S(1)}, u32[]{:S(2)}) copy-start(bf16[512,768]{0,1:T(8,128)(2,1)S(1)} %get-tuple-element.150) | copy-start | bytes 2359300
  311.5 10.7 copy-start.87
  347.0 7.3 copy-start.14
  348.7 5.6 copy-start.16
  375.3 8.9 copy-start.91
  375.3 8.9 copy-start.123
  393.6 9.0 copy-start.19
  393.6 9.0 copy-start.37
  393.6 9.0 copy-start.38
  393.6 9.0 copy-start.84
  393.6 18.7 %slice-start = ((s8[12582912]{0:T(1024)(128)(4,1)}), s8[4194304]{0:T(1024)(128)(4,1)S(1)}, s32[]{:S(2)}) async-start(s8[12582912]{0:T(1024)(128)(4,1)} %bitcast.134), calls=%async_computation.19 | async-start | bytes 8388608
  393.6 18.7 %slice-start.1 = ((s8[12582912]{0:T(1024)(128)(4,1)}), s8[4194304]{0:T(1024)(128)(4,1)S(1)}, s32[]{:S(2)}) async-start(s8[12582912]{0:T(1024)(128)(4,1)} %bitcast.134), calls=%async_computation.20 | async-start | bytes 8388608
  402.6 9.6 slice-start.2
  412.3 7.3 copy-start.17
  448.8 175.1 %all-reduce.13.cloned.1.call-start = ((), (), s32[]{:S(2)}) async-start(), calls=%async_computation.18 | async-start | bytes 4718592
  449.5 5.3 copy-start.53
  457.4 28.6 %copy-start.13 = (f32[512,768]{1,0:T(8,128)S(1)}, f32[512,768]{1,0:T(8,128)}, u32[]{:S(2)}) copy-start(f32[512,768]{1,0:T(8,128)} %copy-done.11) | copy-start | bytes 4718596
  486.0 242.4 %reduce-scatter.15.cloned.1.call-start = ((), (), s32[]{:S(2)}) async-start(), calls=%async_computation.14 | async-start | bytes 2433024 | tf_op jit(solution)/shard_map/reduce_scatter | solution.py:319
  489.4 343.5 %reduce-scatter.21.cloned.1.call-start = ((), (), s32[]{:S(2)}) async-start(), calls=%async_computation.17 | async-start | bytes 2433024
  496.8 460.8 %reduce-scatter.13.cloned.1.call-start = ((), (), s32[]{:S(2)}) async-start(), calls=%async_computation.13 | async-start | bytes 7299072 | tf_op jit(solution)/shard_map/reduce_scatter | solution.py:318
  505.0 594.2 %reduce-scatter.19.cloned.1.call-start = ((), (), s32[]{:S(2)}) async-start(), calls=%async_computation.16 | async-start | bytes 9732096 | tf_op jit(solution)/shard_map/reduce_scatter | solution.py:322
  515.9 725.1 %reduce-scatter.17.cloned.1.call-start = ((), (), s32[]{:S(2)}) async-start(), calls=%async_computation.15 | async-start | bytes 9732096 | tf_op jit(solution)/shard_map/reduce_scatter | solution.py:321
  529.5 8.9 copy-start.113
  529.5 9.8 copy-start.116
  529.5 9.8 copy-start.117
  529.5 51.2 %copy-start.23 = (bf16[768,384]{1,0:T(8,128)(2,1)S(1)}, bf16[768,384]{1,0:T(8,128)(2,1)}, u32[]{:S(2)}) copy-start(bf16[768,384]{1,0:T(8,128)(2,1)} %copy-done.22) | copy-start | bytes 1769476
  529.5 51.2 %copy-start.58 = (f32[16,1152]{1,0:T(8,128)S(1)}, f32[16,1152]{1,0:T(8,128)}, u32[]{:S(2)}) copy-start(f32[16,1152]{1,0:T(8,128)} %copy-done.56) | copy-start | bytes 221188
  529.5 51.5 %copy-start.115 = (f32[16]{0:T(128)S(1)}, f32[16]{0:T(128)}, u32[]{:S(2)}) copy-start(f32[16]{0:T(128)} %copy-done.114) | copy-start | bytes 196
  (99 other events, 208.1 us)
Sparse Core Ops, SparseCore 0:
  10.8 97.2 all-gather.6
  110.9 59.5 all-gather.8
  173.3 53.3 all-gather.10
  229.4 63.4 all-gather.12
  295.6 63.4 all-gather.14
  448.9 33.3 reduce-scatter.10
  488.0 135.8 all-reduce.12
  629.8 98.5 reduce-scatter.14
  734.3 98.6 reduce-scatter.20
  839.0 118.5 reduce-scatter.12
  964.1 135.1 reduce-scatter.18
  1105.6 135.4 reduce-scatter.16
